TPU v7x, 32 devices: a whole 2x2x4 slice. The times are simulated.
32 devices in a mesh: rows: 8 (over z, y), scen: 4 (over x, core).
Axes of the slice: x: 2, y: 2, z: 4, core: 2. Of those that a mesh axis runs over, the one named last changes fastest.
Arguments:
- inverse: bfloat16 [4096, 16384], P('scen', 'rows'), as said below
- voltage_prev: float32 [64, 16384], P('scen', 'rows'), may hold values from -6 to 6
- line_delay: int32 [8, 16], P('rows'), may hold values from 0 to 4, as said below
- line_bus: int32 [8, 16], P('rows'), may hold values from 0 to 2047
- line_impedance: float32 [8, 16], P('rows'), may hold values from 0.5 to 2, as said below
- line_past: float32 [4, 2, 64, 8, 16], P(None, None, 'scen', 'rows'), may hold values from -6 to 6
- model_dest: int32 [1024, 1], P('rows'), may hold values from 0 to 7; in each aligned block of 128 rows (0 to 127, 128 to 255, ...) at most 32 rows name the same one
- model_bus: int32 [1024], P('rows'), may hold values from 0 to 2047
- model_gain: float32 [1024], P('rows'), may hold values from 0.3 to 3
- model_lag: float32 [1024], P('rows'), may hold values from 0.1 to 0.9
- model_state: float32 [64, 1024], P('scen', 'rows'), may hold values from -6 to 6
- model_source: float32 [6, 64, 1024], P(None, 'scen', 'rows'), may hold values from -6 to 6
- switch_bus: int32 [2, 64, 4], P(None, 'scen'), may hold values from 0 to 4095, as said below
- switch_admittance: float32 [64, 4], P('scen'), may hold values from 0.5 to 4
Outputs:
- voltage: float32 [64, 16384], P('scen', 'rows')
- model_current: float32 [64, 1024], P('scen', 'rows')
Inputs may be any that keep to these rules, and one draw needn't show every extreme that they name: `line_delay`: A line joins end (p, q * 2 + c) with end (q, p * 2 + c), with the same delay and impedance at both ends; no line joins the two devices of one subnetwork; delays of lines run from 2 to 4. `line_impedance`: equal at both ends of a line. `switch_bus`: the two buses of a switched branch differ. `inverse`: each block of 4096 columns is symmetric. `model_dest`: among the models of one index of rows at most 32 name the same index.
All inputs are finite; a program needn't handle non-finite values.
Results may differ from a plain program's by a relative error of at most 0.0024.
The roundings to bfloat16 on the way count: a program that leaves them out, or rounds other values in their place, can miss the bound.
Values may be sent and summed in bfloat16 or wider, within the bound.
A program may use at most 128 MiB of HBM per device.

v0:
```python
import jax
import jax.numpy as jnp
from jax import lax
from jax.sharding import PartitionSpec as P


def swapped(value, axis, apart):
    mask = 2**apart
    pairs = [(source, source ^ mask) for source in range(lax.axis_size(axis))]
    return lax.ppermute(value, axis, pairs)


def slot_table(targets, sections, slots):
    onehot = (targets[:, None] == jnp.arange(sections, dtype=jnp.int32)[None, :]).astype(jnp.int32)
    count = targets.shape[0]
    earlier = jnp.arange(count, dtype=jnp.int32)[None, :] < jnp.arange(count, dtype=jnp.int32)[:, None]
    same = targets[:, None] == targets[None, :]
    rank = jnp.sum((earlier & same).astype(jnp.int32), axis=1)
    return targets * slots + rank


def exact_dot(left, right):
    return jnp.dot(left, right, precision=lax.Precision.HIGHEST)


def per_device(
    inverse,
    voltage_prev,
    line_delay,
    line_bus,
    line_impedance,
    line_past,
    model_dest,
    model_bus,
    model_gain,
    model_lag,
    model_state,
    model_source,
    switch_bus,
    switch_admittance,
):
    n = lax.axis_size("rows")
    groups = lax.axis_size("scen")
    place = lax.axis_index("rows")
    share = lax.axis_index("scen")
    subnet = place // 2
    half = place % 2
    lower = half == 0
    depth_rows, width = inverse.shape
    scen = voltage_prev.shape[0]
    steps = model_source.shape[0]
    ends = line_bus.shape[1]
    models = model_bus.shape[0]
    depth_max = line_past.shape[0]
    slots = max(2, 2 * models // n)
    cap = n * slots
    f32, bf16 = jnp.float32, jnp.bfloat16

    def by_half(own, other):
        return jnp.where(lower, jnp.concatenate([own, other], -1), jnp.concatenate([other, own], -1))

    slot = slot_table(model_dest[:, 0], n, slots)
    placing = (slot[:, None] == jnp.arange(cap, dtype=jnp.int32)[None, :]).astype(f32)
    bus_out = exact_dot((model_bus + 1).astype(f32)[None], placing)
    bus_out = jnp.broadcast_to(bus_out.reshape(n // 2, 1, 2 * slots), (n // 2, 2, 2 * slots)).reshape(n, 2 * slots)
    ends_out = jnp.broadcast_to(line_bus.astype(f32) + 1.0, (n, ends))
    buses = lax.all_to_all(jnp.concatenate([bus_out, ends_out], 1), "rows", 0, 0, tiled=True)
    model_pts = buses[:, : 2 * slots].reshape(n, 2, slots).transpose(1, 0, 2).reshape(2, cap)
    ends_pts = lax.dynamic_slice_in_dim(buses[:, 2 * slots :], subnet * 2, 2, axis=0)
    half_pts = jnp.concatenate([model_pts, ends_pts], 1).astype(jnp.int32) - 1
    pts = jnp.where(half_pts < 0, -1, half_pts + jnp.array([[0], [width]], jnp.int32)).reshape(-1)
    own_pts = lax.dynamic_index_in_dim(half_pts, half, 0, keepdims=False)
    hp = cap + ends

    payload = jnp.concatenate(
        [
            model_lag[None],
            ((1.0 - model_lag) * model_gain)[None],
            model_state,
            model_source.reshape(steps * scen, models),
        ],
        0,
    )
    sent = exact_dot(payload, placing).reshape(-1, n // 2, 1, 2 * slots)
    sent = jnp.broadcast_to(sent, (payload.shape[0], n // 2, 2, 2 * slots)).reshape(-1, n, 2 * slots).transpose(1, 0, 2)
    got = lax.all_to_all(sent, "rows", 0, 0, tiled=True)
    got = got.reshape(n, -1, 2, slots).transpose(1, 2, 0, 3).reshape(-1, 2, cap)
    zeros_ends = jnp.zeros((got.shape[0], 2, ends), f32)
    got = jnp.concatenate([got, zeros_ends], 2).reshape(-1, 2 * hp)
    lag, gain, current = got[0], got[1], got[2 : 2 + scen]
    source = got[2 + scen :].reshape(steps, scen, 2 * hp)

    col_sel = (jnp.arange(width, dtype=jnp.int32)[:, None] == own_pts[None, :]).astype(bf16)
    first_all = lax.dynamic_index_in_dim(lax.all_gather(switch_bus[0], "scen", axis=0, tiled=True), subnet, 1, keepdims=False)
    second_all = lax.dynamic_index_in_dim(lax.all_gather(switch_bus[1], "scen", axis=0, tiled=True), subnet, 1, keepdims=False)
    row_ids = jnp.arange(depth_rows, dtype=jnp.int32)[None, :] + share * depth_rows
    col_ids = jnp.arange(width, dtype=jnp.int32)[None, :] + half * width
    picks = (row_ids == first_all[:, None]).astype(bf16) - (row_ids == second_all[:, None]).astype(bf16)
    col_picks = (col_ids == first_all[:, None]).astype(f32) - (col_ids == second_all[:, None]).astype(f32)
    row_sel = (row_ids == pts[:, None]).astype(bf16)
    narrow = jnp.dot(inverse, col_sel, preferred_element_type=f32).astype(bf16)
    part = jnp.dot(row_sel, narrow, preferred_element_type=f32).astype(bf16)
    own_cols = lax.psum(part, "scen")
    branch_part = jnp.dot(picks, inverse, preferred_element_type=f32)
    pts_part = jnp.dot(picks, narrow, preferred_element_type=f32)
    depth_part = jnp.sum(branch_part * col_picks, axis=1, keepdims=True)
    side = lax.psum(jnp.concatenate([pts_part, depth_part], 1), "scen")
    side = lax.dynamic_slice_in_dim(side, share * scen, scen, axis=0)

    own_diag = lax.dynamic_slice_in_dim(own_cols, half * hp, hp, axis=0)
    cross = lax.dynamic_slice_in_dim(own_cols, (1 - half) * hp, hp, axis=0).T
    other_diag = swapped(own_diag, "rows", 0)
    other_cols = jnp.where(lower, jnp.concatenate([cross, other_diag], 0), jnp.concatenate([other_diag, cross], 0))
    matrix = by_half(own_cols, other_cols)

    volt0 = exact_dot(voltage_prev, col_sel.astype(f32))
    past = line_past[:, :, :, 0, :].reshape(depth_max * 2 * scen, ends)
    line_info = jnp.concatenate([past, line_delay.astype(f32), line_impedance], 0)
    other_side = swapped(side, "rows", 0)
    other_volt = swapped(volt0, "rows", 0)
    other_info = swapped(line_info, "rows", 0)
    depth = (side + other_side)[:, hp]
    branch = by_half(side[:, :hp], other_side[:, :hp])
    volt = by_half(volt0, other_volt)
    info = jnp.stack([line_info, other_info])
    info = jnp.where(lower, info, info[::-1])
    past = info[:, : depth_max * 2 * scen].reshape(2, depth_max, 2, scen, ends)
    history = [past[:, k] for k in range(depth_max)]
    delays = info[:, -2][:, None, :]
    impedance = info[:, -1][:, None, :]
    admit = lax.dynamic_index_in_dim(switch_admittance, subnet, axis=1, keepdims=False)

    same = pts[:, None] == pts[None, :]
    before = jnp.arange(2 * hp, dtype=jnp.int32)[:, None] < jnp.arange(2 * hp, dtype=jnp.int32)[None, :]
    leading = jnp.sum((same & before).astype(jnp.int32), axis=0) == 0
    merge = (same & leading[None, :]).astype(f32)

    for step in range(steps):
        current = lag * current + gain * (source[step] - volt)
        line_term = jnp.zeros((2, scen, ends), f32)
        for delay in range(2, depth_max + 1):
            older = history[step - delay + depth_max]
            line_term = line_term + jnp.where(
                delays == delay, -(2.0 / impedance) * older[:, 0] - older[:, 1], 0.0
            )
        zeros = jnp.zeros((scen, cap), f32)
        lines = jnp.concatenate([zeros, line_term[0], zeros, line_term[1]], 1)
        rhs = exact_dot(current - lines, merge).astype(bf16)
        along = jnp.sum(rhs.astype(f32) * branch, axis=1)
        factor = admit * along / (1.0 + admit * depth)
        if step + 1 < steps:
            base = jnp.dot(rhs, matrix, preferred_element_type=f32)
            volt = base - factor[:, None] * branch
        if step + 2 < steps:
            own_volt = jnp.where(lower, volt[:, cap:hp], volt[:, hp + cap :])
            own_term = jnp.where(lower, line_term[0], line_term[1])
            out = jnp.stack([own_volt, own_term]).reshape(2, scen, n // 2, 2 * ends // n)
            out = jnp.broadcast_to(out.transpose(2, 0, 1, 3)[:, None], (n // 2, 2, 2, scen, 2 * ends // n))
            back = lax.all_to_all(out.reshape(n, 2, scen, 2 * ends // n), "rows", 0, 0, tiled=True)
            back = back.reshape(n, 2, scen, 2, ends // n).transpose(3, 1, 2, 0, 4)
            history.append(back.reshape(2, 2, scen, ends))

    rhs_all = lax.all_gather(rhs, "scen", axis=0, tiled=True)
    factor_all = lax.all_gather(factor[:, None], "scen", axis=0, tiled=True)
    dense = jnp.dot(rhs_all, row_sel, preferred_element_type=f32).astype(bf16)
    partial = jnp.dot(dense, inverse, preferred_element_type=f32) - factor_all * branch_part
    voltage = lax.psum_scatter(partial, "scen", scatter_dimension=0, tiled=True)

    own_current = jnp.where(lower, current[:, :cap], current[:, hp : hp + cap])
    back = lax.all_to_all(own_current.reshape(scen, n, slots).transpose(1, 0, 2), "rows", 0, 0, tiled=True)
    model_current = lax.dot_general(
        back.transpose(1, 0, 2).reshape(scen, cap), placing, (((1,), (1,)), ((), ())), precision=lax.Precision.HIGHEST
    )
    return (voltage, model_current)


def solution(mesh):
    placed = (
        P("scen", "rows"),
        P("scen", "rows"),
        P("rows", None),
        P("rows", None),
        P("rows", None),
        P(None, None, "scen", "rows", None),
        P("rows", None),
        P("rows"),
        P("rows"),
        P("rows"),
        P("scen", "rows"),
        P(None, "scen", "rows"),
        P(None, "scen", None),
        P("scen", None),
    )
    return jax.shard_map(
        per_device,
        mesh=mesh,
        in_specs=placed,
        out_specs=(P("scen", "rows"), P("scen", "rows")),
        check_vma=False,
    )
```

profile of v0, /device:TPU:0, one launch (start us, length us, event | category | flops | bytes accessed | tf_op | source)
XLA Modules:
  0.0 226.6 jit_solution(2382398934178793982)
XLA Ops:
  11.1 7.3 %all-to-all-start.1 = ((f32[8,1,80]{2,1,0:T(1,128)}), f32[8,1,80]{2,1,0:T(1,128)S(1)}, u32[]{:S(2)}, u32[]{:S(2)}) async-start(f32[8,1,80]{2,1,0:T(1,128)} %bitcast.19), calls=%async_computation.1 | async-start | bytes 8192 | tf_op jit(solution)/shard_map/all_to_all | solution.py:67
  20.8 2.0 collective-permute-start.1
  23.7 5.2 %all-gather.1 = s32[1,64,4]{2,0,1:T(1,128)S(1)} all-gather(s32[1,16,4]{2,0,1:T(1,128)S(1)} %copy.320), channel_id=3, replica_groups=mesh['rows'=8,'scen'=4] {'scen'}, dimensions={1}, use_global_device_ids=true | all-gather | bytes 1280 | tf_op jit(solution)/shard_map/all_gather | solution.py:95
  29.0 5.2 %all-gather = s32[1,64,4]{2,0,1:T(1,128)S(1)} all-gather(s32[1,16,4]{2,0,1:T(1,128)S(1)} %copy.319), channel_id=2, replica_groups=mesh['rows'=8,'scen'=4] {'scen'}, dimensions={1}, use_global_device_ids=true | all-gather | bytes 1280 | tf_op jit(solution)/shard_map/all_gather | solution.py:94
  34.2 1.3 dynamic-slice_reduce_fusion
  35.5 1.3 dynamic-slice_reduce_fusion.1
  37.5 1.2 fusion.66
  38.7 3.2 %multiply_reduce_fusion = (f32[64]{0:T(128)S(1)}, f32[64,2048]{1,0:T(8,128)S(1)}) fusion(s32[2048]{0:T(1024)S(1)} %iota_add_fusion, s32[64]{0:T(128)S(1)} %dynamic-slice_reduce_fusion, s32[64]{0:T(128)S(1)} %dynamic-slice_reduce_fusion.1, bf16[1024,2048]{1,0:T(8,128)(2,1)} %param.15, s32[1024]{0:T(1024)S(1)} %iota_add_fusion.1), kind=kOutput, calls=%fused_computation.54 | convolution fusion | flops 269680576 | bytes 4731648 | tf_op jit(solution)/shard_map/dot_general | solution.py:104
  44.8 4.5 %all-to-all-start = ((f32[8,114,64]{1,2,0:T(8,128)}), f32[8,114,64]{1,2,0:T(8,128)S(1)}, u32[]{:S(2)}, u32[]{:S(2)}) async-start(f32[8,114,64]{1,2,0:T(8,128)} %bitcast.8), calls=%async_computation | async-start | bytes 524288 | tf_op jit(solution)/shard_map/all_to_all | solution.py:86
  49.7 4.1 %fusion.16 = bf16[272,1024]{1,0:T(8,128)(2,1)S(1)} fusion(bf16[1024,2048]{1,0:T(8,128)(2,1)} %param.15, s32[272]{0:T(512)S(1)} %fusion.142), kind=kOutput, calls=%fused_computation.21 | convolution fusion | flops 1142243328 | bytes 4752448 | tf_op jit(solution)/shard_map/dot_general | solution.py:101
  54.4 1.5 fusion.19
  57.7 2.0 collective-permute-start
  62.9 27.9 %all-reduce.5.cloned.1.call-done = bf16[544,272]{0,1:T(8,128)(2,1)} async-done(((bf16[544,272]{0,1:T(8,128)(2,1)}), bf16[544,272]{0,1:T(8,128)(2,1)}) %all-reduce.5.cloned.1.call-update) | async-done | bytes 295952 | tf_op jit(solution)/shard_map/psum | solution.py:103
  90.7 1.3 constant_dynamic-slice_fusion.4
  92.0 1.5 collective-permute-start.2
  93.6 31.6 %all-reduce.7.cloned.1.call-done = f32[64,273]{1,0:T(8,128)} async-done(((f32[64,273]{1,0:T(8,128)}), f32[64,273]{1,0:T(8,128)}) %all-reduce.7.cloned.1.call-update) | async-done | bytes 69904 | tf_op jit(solution)/shard_map/psum | solution.py:107
  125.9 1.5 collective-permute-start.3
  128.8 1.2 pad_slice_fusion.1
  131.9 1.6 multiply_reduce_fusion.6
  137.3 4.6 %all-to-all-start.3 = ((f32[8,1,128]{2,1,0:T(1,128)}), f32[8,1,128]{2,1,0:T(1,128)S(1)}, u32[]{:S(2)}, u32[]{:S(2)}) async-start(f32[8,1,128]{2,1,0:T(1,128)} %reshape.252), calls=%async_computation.3 | async-start | bytes 8192 | tf_op jit(solution)/shard_map/all_to_all | solution.py:159
  143.1 5.2 %all-to-all-done.3 = f32[8,1,128]{2,1,0:T(1,128)S(1)} async-done(((f32[8,1,128]{2,1,0:T(1,128)}), f32[8,1,128]{2,1,0:T(1,128)S(1)}, u32[]{:S(2)}, u32[]{:S(2)}) %all-to-all-start.3) | async-done | bytes 4128 | tf_op jit(solution)/shard_map/all_to_all | solution.py:159
  148.3 3.3 %all-to-all-start.2 = ((f32[8,1,128]{2,1,0:T(1,128)}), f32[8,1,128]{2,1,0:T(1,128)S(1)}, u32[]{:S(2)}, u32[]{:S(2)}) async-start(f32[8,1,128]{2,1,0:T(1,128)} %reshape.250), calls=%async_computation.2 | async-start | bytes 8192 | tf_op jit(solution)/shard_map/all_to_all | solution.py:159
  153.2 4.7 %all-to-all-done.2 = f32[8,1,128]{2,1,0:T(1,128)S(1)} async-done(((f32[8,1,128]{2,1,0:T(1,128)}), f32[8,1,128]{2,1,0:T(1,128)S(1)}, u32[]{:S(2)}, u32[]{:S(2)}) %all-to-all-start.2) | async-done | bytes 4128 | tf_op jit(solution)/shard_map/all_to_all | solution.py:159
  162.5 3.3 %all-to-all-start.5 = ((f32[8,1,128]{2,1,0:T(1,128)}), f32[8,1,128]{2,1,0:T(1,128)S(1)}, u32[]{:S(2)}, u32[]{:S(2)}) async-start(f32[8,1,128]{2,1,0:T(1,128)} %reshape.256), calls=%async_computation.5 | async-start | bytes 8192 | tf_op jit(solution)/shard_map/all_to_all | solution.py:159
  166.7 5.5 %all-to-all-done.5 = f32[8,1,128]{2,1,0:T(1,128)S(1)} async-done(((f32[8,1,128]{2,1,0:T(1,128)}), f32[8,1,128]{2,1,0:T(1,128)S(1)}, u32[]{:S(2)}, u32[]{:S(2)}) %all-to-all-start.5) | async-done | bytes 4128 | tf_op jit(solution)/shard_map/all_to_all | solution.py:159
  172.2 3.3 %all-to-all-start.4 = ((f32[8,1,128]{2,1,0:T(1,128)}), f32[8,1,128]{2,1,0:T(1,128)S(1)}, u32[]{:S(2)}, u32[]{:S(2)}) async-start(f32[8,1,128]{2,1,0:T(1,128)} %reshape.254), calls=%async_computation.4 | async-start | bytes 8192 | tf_op jit(solution)/shard_map/all_to_all | solution.py:159
  176.5 5.3 %all-to-all-done.4 = f32[8,1,128]{2,1,0:T(1,128)S(1)} async-done(((f32[8,1,128]{2,1,0:T(1,128)}), f32[8,1,128]{2,1,0:T(1,128)S(1)}, u32[]{:S(2)}, u32[]{:S(2)}) %all-to-all-start.4) | async-done | bytes 4128 | tf_op jit(solution)/shard_map/all_to_all | solution.py:159
  184.9 5.3 %all_gather.14 = bf16[64,544]{1,0:T(8,128)(2,1)S(1)} all-gather(bf16[16,544]{1,0:T(8,128)(2,1)S(1)} %get-tuple-element.76), channel_id=1, replica_groups=mesh['rows'=8,'scen'=4] {'scen'}, dimensions={0}, use_global_device_ids=true | all-gather | bytes 87040 | tf_op jit(solution)/shard_map/all_gather | solution.py:163
  190.6 6.1 %all-reduce.1 = f32[64]{0:T(128)S(1)} all-reduce(f32[64]{0:T(128)S(1)} %dynamic-update-slice), channel_id=1, replica_groups=mesh['rows'=8,'scen'=4] {'scen'}, use_global_device_ids=true, to_apply=%add.1 | all-reduce | flops 64 | bytes 512
  196.7 4.3 %convolution_subtract_fusion = f32[64,2048]{1,0:T(8,128)} fusion(bf16[1024,2048]{1,0:T(8,128)(2,1)} %param.15, bf16[64,544]{1,0:T(8,128)(2,1)S(1)} %all_gather.14, s32[1024]{0:T(1024)S(1)} %iota_add_fusion.1, s32[544]{0:T(1024)S(1)} %select_n.202, f32[64,2048]{1,0:T(8,128)S(1)} %get-tuple-element.65, f32[64]{0:T(128)S(1)} %all-reduce.1), kind=kOutput, calls=%fused_computation.7 | convolution fusion | flops 340623360 | bytes 5319040 | tf_op jit(solution)/shard_map/dot_general | solution.py:166
  201.3 8.9 %all_to_all.42 = f32[8,1,512]{2,1,0:T(1,128)S(1)} all-to-all(f32[8,1,512]{2,1,0:T(1,128)S(1)} %reshape.258), channel_id=1, replica_groups=mesh['rows'=8,'scen'=4] {'rows'}, dimensions={0} | all-to-all | bytes 32768 | tf_op jit(solution)/shard_map/all_to_all | solution.py:170
  212.0 8.1 %reduce-scatter.2.cloned.1.call-done = f32[16,2048]{1,0:T(8,128)} async-done(((f32[64,2048]{1,0:T(8,128)}), f32[16,2048]{1,0:T(8,128)}) %reduce-scatter.2.cloned.1.call-update) | async-done | bytes 131088 | tf_op jit(solution)/shard_map/reduce_scatter | solution.py:167
  (194 shorter events, 38.4 us)
Async XLA Ops:
  7.2 48.7 %copy-start = (f32[16,2048]{1,0:T(8,128)S(1)}, f32[16,2048]{1,0:T(8,128)}, u32[]{:S(2)}) copy-start(f32[16,2048]{1,0:T(8,128)} %param.16) | copy-start | bytes 393220
  8.8 33.1 %copy-start.4 = (s32[128]{0:T(128)}, s32[128]{0:T(128)S(1)}, u32[]{:S(2)}) copy-start(s32[128]{0:T(128)S(1)} %fusion.143) | copy-start | bytes 1540
  11.1 32.9 %all-to-all-start.1 = ((f32[8,1,80]{2,1,0:T(1,128)}), f32[8,1,80]{2,1,0:T(1,128)S(1)}, u32[]{:S(2)}, u32[]{:S(2)}) async-start(f32[8,1,80]{2,1,0:T(1,128)} %bitcast.19), calls=%async_computation.1 | async-start | bytes 8192 | tf_op jit(solution)/shard_map/all_to_all | solution.py:67
  20.8 39.7 %collective-permute-start.1 = (f32[130,16]{0,1:T(8,128)S(1)}, f32[130,16]{0,1:T(8,128)S(1)}, u32[]{:S(2)}, u32[]{:S(2)}) collective-permute-start(f32[130,16]{0,1:T(8,128)S(1)} %pad_maximum_fusion.14), channel_id=1, source_target_pairs={{0,4},{4,0},{8,12},{12,8},{16,20},{20,16},{24,28},{28,24},{1,5},{5... | collective-permute-start | bytes 24968 | tf_op jit(solution)/shard_map/ppermute | solution.py:10
  38.7 4.1 %copy-start.6 = (u32[32]{0:T(128)S(1)}, u32[32]{0:T(128)}, u32[]{:S(2)}) copy-start(u32[32]{0:T(128)} %constant.102) | copy-start | bytes 388
  44.8 84.1 %all-to-all-start = ((f32[8,114,64]{1,2,0:T(8,128)}), f32[8,114,64]{1,2,0:T(8,128)S(1)}, u32[]{:S(2)}, u32[]{:S(2)}) async-start(f32[8,114,64]{1,2,0:T(8,128)} %bitcast.8), calls=%async_computation | async-start | bytes 524288 | tf_op jit(solution)/shard_map/all_to_all | solution.py:86
  49.3 41.4 %all-reduce.5.cloned.1.call-start = ((), (), s32[]{:S(2)}) async-start(), calls=%async_computation.8 | async-start | bytes 696320 | tf_op jit(solution)/shard_map/psum | solution.py:103
  56.9 68.2 %all-reduce.7.cloned.1.call-start = ((), (), s32[]{:S(2)}) async-start(), calls=%async_computation.9 | async-start | bytes 196608 | tf_op jit(solution)/shard_map/psum | solution.py:107
  57.7 74.1 %collective-permute-start = (f32[16,272]{1,0:T(8,128)S(1)}, f32[16,272]{1,0:T(8,128)S(1)}, u32[]{:S(2)}, u32[]{:S(2)}) collective-permute-start(f32[16,272]{1,0:T(8,128)S(1)} %fusion.39), channel_id=1, source_target_pairs={{0,4},{4,0},{8,12},{12,8},{16,20},{20,16},{24,28},{28,24},{1,5},{5... | collective-permute-start | bytes 52232 | tf_op jit(solution)/shard_map/ppermute | solution.py:10
  90.7 37.8 %copy-start.1 = (bf16[544,272]{0,1:T(8,128)(2,1)S(1)}, bf16[544,272]{0,1:T(8,128)(2,1)}, u32[]{:S(2)}) copy-start(bf16[544,272]{0,1:T(8,128)(2,1)} %all-reduce.5.cloned.1.call-done) | copy-start | bytes 887812
  92.0 36.2 %collective-permute-start.2 = (bf16[272,272]{0,1:T(8,128)(2,1)S(1)}, bf16[272,272]{0,1:T(8,128)(2,1)S(1)}, u32[]{:S(2)}, u32[]{:S(2)}) collective-permute-start(bf16[272,272]{0,1:T(8,128)(2,1)S(1)} %get-tuple-element.22), channel_id=1, source_target_pairs={{0,4},{4,0},{8,12},{12,8},{16,20},{20,16},{24,28},{28,24},{1,5},{5... | collective-permute-start | bytes 443912 | tf_op jit(solution)/shard_map/ppermute | solution.py:10
  125.9 6.0 %collective-permute-start.3 = (f32[16,273]{1,0:T(8,128)S(1)}, f32[16,273]{1,0:T(8,128)}, u32[]{:S(2)}, u32[]{:S(2)}) collective-permute-start(f32[16,273]{1,0:T(8,128)S(1)} %constant_dynamic-slice_fusion), channel_id=1, source_target_pairs={{0,4},{4,0},{8,12},{12,8},{16,20},{20,16},{24,28},{28,24},{1,5},{5... | collective-permute-start | bytes 52424 | tf_op jit(solution)/shard_map/ppermute | solution.py:10
  131.3 3.9 %copy-start.2 = (f32[16,16]{1,0:T(8,128)S(1)}, f32[16,16]{1,0:T(8,128)}, u32[]{:S(2)}) copy-start(f32[16,16]{1,0:T(8,128)} %get-tuple-element.59) | copy-start | bytes 3076
  131.3 3.9 %copy-start.3 = (pred[544]{0:T(1024)(128)(4,1)S(1)}, pred[544]{0:T(1024)(128)(4,1)}, u32[]{:S(2)}) copy-start(pred[544]{0:T(1024)(128)(4,1)} %broadcast_compare_fusion) | copy-start | bytes 1636
  137.3 11.0 %all-to-all-start.3 = ((f32[8,1,128]{2,1,0:T(1,128)}), f32[8,1,128]{2,1,0:T(1,128)S(1)}, u32[]{:S(2)}, u32[]{:S(2)}) async-start(f32[8,1,128]{2,1,0:T(1,128)} %reshape.252), calls=%async_computation.3 | async-start | bytes 8192 | tf_op jit(solution)/shard_map/all_to_all | solution.py:159
  148.3 9.6 %all-to-all-start.2 = ((f32[8,1,128]{2,1,0:T(1,128)}), f32[8,1,128]{2,1,0:T(1,128)S(1)}, u32[]{:S(2)}, u32[]{:S(2)}) async-start(f32[8,1,128]{2,1,0:T(1,128)} %reshape.250), calls=%async_computation.2 | async-start | bytes 8192 | tf_op jit(solution)/shard_map/all_to_all | solution.py:159
  162.5 9.6 %all-to-all-start.5 = ((f32[8,1,128]{2,1,0:T(1,128)}), f32[8,1,128]{2,1,0:T(1,128)S(1)}, u32[]{:S(2)}, u32[]{:S(2)}) async-start(f32[8,1,128]{2,1,0:T(1,128)} %reshape.256), calls=%async_computation.5 | async-start | bytes 8192 | tf_op jit(solution)/shard_map/all_to_all | solution.py:159
  172.2 9.6 %all-to-all-start.4 = ((f32[8,1,128]{2,1,0:T(1,128)}), f32[8,1,128]{2,1,0:T(1,128)S(1)}, u32[]{:S(2)}, u32[]{:S(2)}) async-start(f32[8,1,128]{2,1,0:T(1,128)} %reshape.254), calls=%async_computation.4 | async-start | bytes 8192 | tf_op jit(solution)/shard_map/all_to_all | solution.py:159
  175.5 44.6 %reduce-scatter.2.cloned.1.call-start = ((), (), s32[]{:S(2)}) async-start(), calls=%async_computation.10 | async-start | bytes 655360 | tf_op jit(solution)/shard_map/reduce_scatter | solution.py:167
  196.7 14.5 %copy-start.5 = (s32[128]{0:T(128)S(1)}, s32[128]{0:T(128)}, u32[]{:S(2)}) copy-start(s32[128]{0:T(128)} %copy-done.4) | copy-start | bytes 1540
Sparse Core Ops, SparseCore 0:
  57.1 33.6 all-reduce.4
  93.6 31.4 all-reduce.6
  201.1 18.9 reduce-scatter.1
where the time goes:
time: 228 us; the launch traced here: 227 us
  waiting for transfers between devices  88.3 us (39%)
  starting transfers between devices  33.7 us (15%)
  blocking collectives  30.7 us (13%)
  matrix products  24.3 us (11%)
  local copies, waits for them, and re-layouts  21.1 us (9%)
  between operations  15 us (7%)
  other arithmetic  13.6 us (6%)
    psum x1, waiting for transfers between devices, per_device(): side = lax.psum(jnp.concatenate([pts_part, depth_part], 1), 'scen')  31.6 us
    psum x1, waiting for transfers between devices, per_device(): own_cols = lax.psum(part, 'scen')  27.9 us
    all_to_all x4, waiting for transfers between devices, per_device(): lax.all_to_all(out.reshape(n, 2, scen, 2 * ends // n), 'rows', 0, 0, tile...  20.7 us
    all_to_all x4, starting transfers between devices, per_device(): lax.all_to_all(out.reshape(n, 2, scen, 2 * ends // n), 'rows', 0, 0, tile...  14.5 us
    all_to_all x1, blocking collectives, per_device(): lax.all_to_all(own_current.reshape(scen, n, slots).transpose(1, 0, 2), 'r...  8.94 us
    dot_general x9, matrix products, exact_dot(): return jnp.dot(left, right, precision=lax.Precision.HIGHEST)  8.49 us
    reduce_scatter x1, waiting for transfers between devices, per_device(): voltage = lax.psum_scatter(partial, 'scen', scatter_dimension=0, tiled=True)  8.07 us
    all_to_all x1, starting transfers between devices, per_device(): lax.all_to_all(jnp.concatenate([bus_out, ends_out], 1), 'rows', 0, 0, til...  7.28 us
  transfers between devices with their start and end apart: 13, of which 7 were waited for; matrix products, arithmetic and copies ran while one was open for 17% of the time, Pallas kernels for 0%

commit v1 on v0

v1 whole, which is shorter than its diff:
```python
import functools

import jax
import jax.numpy as jnp
from jax import lax
from jax.experimental import pallas as pl
from jax.experimental.pallas import tpu as pltpu
from jax.sharding import PartitionSpec as P


def slot_table(targets, sections, slots):
    onehot = (targets[:, None] == jnp.arange(sections, dtype=jnp.int32)[None, :]).astype(jnp.int32)
    count = targets.shape[0]
    earlier = jnp.arange(count, dtype=jnp.int32)[None, :] < jnp.arange(count, dtype=jnp.int32)[:, None]
    same = targets[:, None] == targets[None, :]
    rank = jnp.sum((earlier & same).astype(jnp.int32), axis=1)
    return targets * slots + rank


def exact_dot(left, right):
    return jnp.dot(left, right, precision=lax.Precision.HIGHEST)


def split_dot(value, selector):
    rows = value.shape[0]
    high = value.astype(jnp.bfloat16)
    rest = value - high.astype(jnp.float32)
    middle = rest.astype(jnp.bfloat16)
    low = (rest - middle.astype(jnp.float32)).astype(jnp.bfloat16)
    stacked = jnp.concatenate([high, middle, low], 0)
    out = jnp.dot(stacked, selector, preferred_element_type=jnp.float32)
    return out[:rows] + out[rows : 2 * rows] + out[2 * rows :]


def step_kernel(
    n,
    groups,
    steps,
    depth_max,
    cap,
    part_ref,
    side_ref,
    volt_ref,
    info_ref,
    rates_ref,
    state_ref,
    source_ref,
    merge_ref,
    row_sel_ref,
    perm_ref,
    end_sub_ref,
    admit_ref,
    inverse_ref,
    branch_part_ref,
    home_ref,
    voltage_ref,
    current_ref,
    part_in,
    side_in,
    matrix,
    volt_in,
    info_in,
    line_out,
    line_in,
    feed_out,
    feed_in,
    factor_out,
    factor_in,
    partial_out,
    partial_in,
    state_out,
    state_in,
    group_sems,
    pair_sems,
    line_sems,
    last_sems,
    home_sems,
):
    f32, bf16 = jnp.float32, jnp.bfloat16
    place = lax.axis_index("rows")
    share = lax.axis_index("scen")
    subs = n // 2
    subnet, half = place // 2, place % 2
    base_row = subnet * 2
    size = 2 * groups
    me = half * groups + share
    scen = state_ref.shape[0]
    points = matrix.shape[0]
    block = points // size
    lower = half == 0

    def member(index):
        return (base_row + index // groups, index % groups)

    def remote(src, dst, sems, device):
        return pltpu.make_async_remote_copy(
            src_ref=src,
            dst_ref=dst,
            send_sem=sems.at[0],
            recv_sem=sems.at[1],
            device_id=device,
            device_id_type=pl.DeviceIdType.MESH,
        )

    barrier = pltpu.get_barrier_semaphore()
    for d in range(1, size):
        pl.semaphore_signal(
            barrier, inc=1, device_id=member((me + d) % size), device_id_type=pl.DeviceIdType.MESH
        )
    for d in range(1, subs):
        for other in range(2):
            device = (((subnet + d) % subs) * 2 + other, share)
            pl.semaphore_signal(barrier, inc=1, device_id=device, device_id_type=pl.DeviceIdType.MESH)
    pl.semaphore_wait(barrier, size - 1 + 2 * (subs - 1))

    first = []
    for d in range(1, size):
        peer = (me + d) % size
        rows = pl.ds(pl.multiple_of(peer * block, 16), block)
        first.append(remote(part_ref.at[rows], part_in.at[d - 1], group_sems.at[0, d], member(peer)))
    for copy in first:
        copy.start()
    pair = ((place // 2) * 2 + (1 - half), share)
    pairs = [
        remote(volt_ref, volt_in, pair_sems.at[0], pair),
        remote(info_ref, info_in, pair_sems.at[1], pair),
    ]
    for copy in pairs:
        copy.start()
    sides = []
    for d in range(1, size):
        peer = (me + d) % size
        rows = pl.ds(pl.multiple_of((peer % groups) * scen, 8), scen)
        sides.append(remote(side_ref.at[rows], side_in.at[d - 1], group_sems.at[1, d], member(peer)))
    for copy in sides:
        copy.start()
    own_rows = pl.ds(pl.multiple_of(me * block, 16), block)

    def placed(pieces):
        lows = jnp.zeros_like(pieces[0][1][:, :cap])
        highs = jnp.zeros_like(lows)
        rest = jnp.zeros_like(pieces[0][1][:, cap:])
        for from_lower, piece in pieces:
            lows = lows + jnp.where(from_lower, piece[:, :cap], 0.0)
            highs = highs + jnp.where(from_lower, 0.0, piece[:, :cap])
            rest = rest + piece[:, cap:]
        return lows, highs, rest

    pieces = [(lower, part_ref[own_rows, :].astype(f32))]
    for d in range(1, size):
        first[d - 1].wait()
        pieces.append(((me + size - d) % size < groups, part_in[d - 1].astype(f32)))
    matrix[own_rows, :] = jnp.concatenate(placed(pieces), 1).astype(bf16)
    second = []
    for d in range(1, size):
        second.append(
            remote(matrix.at[own_rows], matrix.at[own_rows], group_sems.at[2, d], member((me + d) % size))
        )
    for copy in second:
        copy.start()

    pieces = [(lower, side_ref[pl.ds(pl.multiple_of(share * scen, 8), scen), :])]
    for d in range(1, size):
        sides[d - 1].wait()
        pieces.append(((me + size - d) % size < groups, side_in[d - 1]))
    lows, highs, rest = placed(pieces)
    ends = perm_ref.shape[0]
    branch = jnp.concatenate([lows, highs, rest[:, :ends]], 1)
    depth = rest[:, ends : ends + 1]
    for copy in pairs:
        copy.wait()
    own_volt, other_volt = volt_ref[...], volt_in[...]
    volt = jnp.concatenate(
        [jnp.where(lower, own_volt, other_volt), jnp.where(lower, other_volt, own_volt)], 1
    )
    past_rows = depth_max * 2 * scen
    info = info_ref[...] + info_in[...]
    delays = info[past_rows : past_rows + 1]
    impedance = info[past_rows + 1 : past_rows + 2]
    admittance = 2.0 / jnp.where(delays == 0.0, 1.0, impedance)
    history = [info[k * 2 * scen : (k + 1) * 2 * scen] for k in range(depth_max)]
    lag, gain = rates_ref[0:1, :], rates_ref[1:2, :]
    admit = admit_ref[:, 0:1]
    current = state_ref[...]
    lines = []
    homes = []
    for step in range(steps):
        current = lag * current + gain * (source_ref[step] - volt)
        if step + 1 == steps:
            state_out[...] = jnp.where(lower, current[:, :cap], current[:, cap:])
            for d in range(1, n):
                homes.append(
                    remote(state_out, state_in.at[d - 1], home_sems.at[d], ((place + d) % n, share))
                )
            for copy in homes:
                copy.start()
        if step >= 2:
            for copy in lines[step - 2]:
                copy.wait()
            merged = jnp.zeros((2 * scen, ends), f32)
            for d in range(1, subs):
                moved = split_dot(line_in[step - 2, d - 1], perm_ref[...])
                merged = merged + jnp.where(end_sub_ref[0:1, :] == (subnet + subs - d) % subs, moved, 0.0)
            history.append(merged)
        line_term = jnp.zeros((scen, ends), f32)
        for delay in range(2, depth_max + 1):
            older = history[step - delay + depth_max]
            line_term = line_term + jnp.where(
                delays == delay, -admittance * older[:scen] - older[scen:], 0.0
            )
        feed = split_dot(jnp.concatenate([current, -line_term], 1), merge_ref[...])
        rhs = feed.astype(bf16)
        along = jnp.sum(rhs.astype(f32) * branch, axis=1, keepdims=True)
        factor = admit * along / (1.0 + admit * depth)
        if step == 0:
            for copy in second:
                copy.wait()
        if step + 1 < steps:
            full = jnp.dot(rhs, matrix[...], preferred_element_type=f32) - factor * branch
            volt = full[:, : 2 * cap]
        if step + 2 < steps:
            line_out[step] = jnp.concatenate([full[:, 2 * cap :], line_term], 0)
            lines.append(
                [
                    remote(
                        line_out.at[step],
                        line_in.at[step, d - 1],
                        line_sems.at[step, d],
                        (((subnet + d) % subs) * 2 + half, share),
                    )
                    for d in range(1, subs)
                ]
            )
            for copy in lines[step]:
                copy.start()

    feed_out[...] = rhs
    factor_out[...] = jnp.broadcast_to(factor, factor_out.shape)
    shared = []
    for d in range(1, groups):
        device = (place, (share + d) % groups)
        shared.append(remote(feed_out, feed_in.at[d - 1], last_sems.at[0, d], device))
        shared.append(remote(factor_out, factor_in.at[d - 1], last_sems.at[1, d], device))
    for copy in shared:
        copy.start()
    for copy in shared:
        copy.wait()
    feeds = jnp.concatenate([feed_in[d - 1] for d in range(1, groups)] + [rhs], 0)
    dense = jnp.dot(feeds, row_sel_ref[...], preferred_element_type=f32).astype(bf16)
    width = inverse_ref.shape[1]
    tile = min(width, 512)
    for at in range(0, width, tile):
        product = jnp.dot(dense, inverse_ref[:, at : at + tile], preferred_element_type=f32)
        for d in range(1, groups):
            rows = pl.ds(pl.multiple_of(((share + groups - d) % groups) * scen, 8), scen)
            partial_out[d - 1, :, at : at + tile] = (
                product[(d - 1) * scen : d * scen]
                - factor_in[d - 1][:, 0:1] * branch_part_ref[rows, at : at + tile]
            )
        rows = pl.ds(pl.multiple_of(share * scen, 8), scen)
        voltage_ref[:, at : at + tile] = (
            product[(groups - 1) * scen :] - factor * branch_part_ref[rows, at : at + tile]
        )
    partials = []
    for d in range(1, groups):
        device = (place, (share + groups - d) % groups)
        partials.append(remote(partial_out.at[d - 1], partial_in.at[d - 1], last_sems.at[2, d], device))
    for copy in partials:
        copy.start()
    for copy in homes:
        copy.wait()
    out = split_dot(state_out[...], home_ref[0])
    for d in range(1, n):
        out = out + split_dot(state_in[d - 1], home_ref[d])
    current_ref[...] = out
    for copy in partials:
        copy.wait()
    total = voltage_ref[...]
    for d in range(1, groups):
        total = total + partial_in[d - 1]
    voltage_ref[...] = total


def per_device(
    inverse,
    voltage_prev,
    line_delay,
    line_bus,
    line_impedance,
    line_past,
    model_dest,
    model_bus,
    model_gain,
    model_lag,
    model_state,
    model_source,
    switch_bus,
    switch_admittance,
):
    n = lax.axis_size("rows")
    groups = lax.axis_size("scen")
    place = lax.axis_index("rows")
    share = lax.axis_index("scen")
    subnet = place // 2
    half = place % 2
    lower = half == 0
    depth_rows, width = inverse.shape
    scen = voltage_prev.shape[0]
    steps = model_source.shape[0]
    ends = line_bus.shape[1]
    models = model_bus.shape[0]
    depth_max = line_past.shape[0]
    slots = max(2, 2 * models // n)
    cap = n * slots
    f32, bf16 = jnp.float32, jnp.bfloat16

    pad = max(128, 2 * ends)
    points = 2 * cap + pad

    def end_lanes(values):
        none = jnp.zeros((values.shape[0], ends), values.dtype)
        both = jnp.where(
            lower, jnp.concatenate([values, none], 1), jnp.concatenate([none, values], 1)
        )
        return jnp.pad(both, ((0, 0), (0, pad - 2 * ends)))

    slot = slot_table(model_dest[:, 0], n, slots)
    placing = (slot[:, None] == jnp.arange(cap, dtype=jnp.int32)[None, :]).astype(f32)
    bus_out = exact_dot((model_bus + 1).astype(f32)[None], placing)
    bus_out = jnp.broadcast_to(bus_out.reshape(n // 2, 1, 2 * slots), (n // 2, 2, 2 * slots)).reshape(n, 2 * slots)
    ends_out = jnp.broadcast_to(line_bus.astype(f32) + 1.0, (n, ends))
    buses = lax.all_to_all(jnp.concatenate([bus_out, ends_out], 1), "rows", 0, 0, tiled=True)
    model_pts = buses[:, : 2 * slots].reshape(n, 2, slots).transpose(1, 0, 2).reshape(2, cap)
    ends_pts = lax.dynamic_slice_in_dim(buses[:, 2 * slots :], subnet * 2, 2, axis=0)
    model_pts = model_pts.astype(jnp.int32) - 1
    ends_pts = ends_pts.astype(jnp.int32) - 1
    shift = jnp.array([[0], [width]], jnp.int32)
    pts = jnp.concatenate(
        [
            jnp.where(model_pts < 0, -1, model_pts + shift).reshape(-1),
            (ends_pts + shift).reshape(-1),
            jnp.full((pad - 2 * ends,), -1, jnp.int32),
        ]
    )
    own_models = lax.dynamic_index_in_dim(model_pts, half, 0, keepdims=False)
    own_pts = jnp.concatenate([own_models, end_lanes(line_bus + 1)[0] - 1])

    payload = jnp.concatenate(
        [
            model_lag[None],
            ((1.0 - model_lag) * model_gain)[None],
            jnp.zeros((6, models), f32),
            model_state,
            model_source.reshape(steps * scen, models),
        ],
        0,
    )
    count = payload.shape[0]
    sent = exact_dot(payload, placing).reshape(-1, n // 2, 1, 2 * slots)
    sent = jnp.broadcast_to(sent, (count, n // 2, 2, 2 * slots)).reshape(-1, n, 2 * slots).transpose(1, 0, 2)
    got = lax.all_to_all(sent, "rows", 0, 0, tiled=True)
    got = got.reshape(n, -1, 2, slots).transpose(1, 2, 0, 3).reshape(-1, 2 * cap)
    rates, state = got[:8], got[8 : 8 + scen]
    source = got[8 + scen :].reshape(steps, scen, 2 * cap)

    col_sel = (jnp.arange(width, dtype=jnp.int32)[:, None] == own_pts[None, :]).astype(bf16)
    switches = lax.all_gather(switch_bus, "scen", axis=1, tiled=True)
    switches = lax.dynamic_index_in_dim(switches, subnet, 2, keepdims=False)
    row_ids = jnp.arange(depth_rows, dtype=jnp.int32)[None, :] + share * depth_rows
    col_ids = jnp.arange(width, dtype=jnp.int32)[None, :] + half * width
    picks = (row_ids == switches[0][:, None]).astype(bf16) - (row_ids == switches[1][:, None]).astype(bf16)
    col_picks = (col_ids == switches[0][:, None]).astype(f32) - (col_ids == switches[1][:, None]).astype(f32)
    row_sel = (row_ids == pts[:, None]).astype(bf16)
    narrow = jnp.dot(inverse, col_sel, preferred_element_type=f32).astype(bf16)
    part = jnp.dot(row_sel, narrow, preferred_element_type=f32).astype(bf16)
    branch_part = jnp.dot(picks, inverse, preferred_element_type=f32)
    pts_part = jnp.dot(picks, narrow, preferred_element_type=f32)
    depth_part = jnp.sum(branch_part * col_picks, axis=1, keepdims=True)
    side = jnp.concatenate([pts_part, jnp.broadcast_to(depth_part, (depth_part.shape[0], 128))], 1)
    volt0 = exact_dot(voltage_prev, col_sel[:, :cap].astype(f32))
    past = line_past[:, :, :, 0, :].reshape(depth_max * 2 * scen, ends)
    info = end_lanes(
        jnp.concatenate([past, line_delay.astype(f32), line_impedance, jnp.zeros((6, ends), f32)], 0)
    )
    same = pts[:, None] == pts[None, :]
    before = jnp.arange(points, dtype=jnp.int32)[:, None] < jnp.arange(points, dtype=jnp.int32)[None, :]
    leading = jnp.sum((same & before).astype(jnp.int32), axis=0) == 0
    merge = (same & leading[None, :]).astype(bf16)

    per_pair = ends // n
    lane = jnp.arange(pad, dtype=jnp.int32)
    lane_half, slot_at = lane // ends, lane % ends
    partner = slot_at // per_pair
    origin = (partner % 2) * ends + (2 * subnet + lane_half) * per_pair + slot_at % per_pair
    perm = ((jnp.arange(pad, dtype=jnp.int32)[:, None] == origin[None, :]) & (lane < 2 * ends)[None, :]).astype(bf16)
    end_sub = jnp.broadcast_to((partner // 2)[None], (8, pad))
    admit = lax.dynamic_index_in_dim(switch_admittance, subnet, axis=1, keepdims=False)
    admit = jnp.broadcast_to(admit[:, None], (scen, 128))
    rank = slot % slots
    target = (place - jnp.arange(n, dtype=jnp.int32)) % n
    home = (
        (model_dest[:, 0][None, None, :] == target[:, None, None])
        & (jnp.arange(cap, dtype=jnp.int32)[None, :, None] == (place * slots + rank)[None, None, :])
    ).astype(bf16)

    size = 2 * groups
    cols = cap + pad
    vmem = pl.BlockSpec(memory_space=pltpu.VMEM)
    voltage, model_current = pl.pallas_call(
        functools.partial(step_kernel, n, groups, steps, depth_max, cap),
        out_shape=(
            jax.ShapeDtypeStruct((scen, width), f32),
            jax.ShapeDtypeStruct((scen, models), f32),
        ),
        in_specs=[vmem] * 15,
        out_specs=(vmem, vmem),
        scratch_shapes=[
            pltpu.VMEM((size - 1, points // size, cols), bf16),
            pltpu.VMEM((size - 1, scen, cols + 128), f32),
            pltpu.VMEM((points, points), bf16),
            pltpu.VMEM((scen, cap), f32),
            pltpu.VMEM(info.shape, f32),
            pltpu.VMEM((steps - 2, 2 * scen, pad), f32),
            pltpu.VMEM((steps - 2, n // 2 - 1, 2 * scen, pad), f32),
            pltpu.VMEM((scen, points), bf16),
            pltpu.VMEM((groups - 1, scen, points), bf16),
            pltpu.VMEM((scen, 128), f32),
            pltpu.VMEM((groups - 1, scen, 128), f32),
            pltpu.VMEM((groups - 1, scen, width), f32),
            pltpu.VMEM((groups - 1, scen, width), f32),
            pltpu.VMEM((scen, cap), f32),
            pltpu.VMEM((n - 1, scen, cap), f32),
            pltpu.SemaphoreType.DMA((3, size, 2)),
            pltpu.SemaphoreType.DMA((2, 2)),
            pltpu.SemaphoreType.DMA((steps - 2, n // 2, 2)),
            pltpu.SemaphoreType.DMA((3, groups, 2)),
            pltpu.SemaphoreType.DMA((n, 2)),
        ],
        compiler_params=pltpu.CompilerParams(
            collective_id=0, has_side_effects=True, vmem_limit_bytes=56 * 2**20
        ),
    )(
        part, side, volt0, info, rates, state, source, merge, row_sel, perm, end_sub, admit,
        inverse, branch_part, home,
    )
    return (voltage, model_current)


def solution(mesh):
    placed = (
        P("scen", "rows"),
        P("scen", "rows"),
        P("rows", None),
        P("rows", None),
        P("rows", None),
        P(None, None, "scen", "rows", None),
        P("rows", None),
        P("rows"),
        P("rows"),
        P("rows"),
        P("scen", "rows"),
        P(None, "scen", "rows"),
        P(None, "scen", None),
        P("scen", None),
    )
    return jax.shard_map(
        per_device,
        mesh=mesh,
        in_specs=placed,
        out_specs=(P("scen", "rows"), P("scen", "rows")),
        check_vma=False,
    )
```

time: 228 us -> 112 us (0.49)
  waiting for transfers between devices: 88.3 us -> 0.01 us
  Pallas kernels: 0 us -> 50.8 us
  blocking collectives: 30.7 us -> 5.25 us
  starting transfers between devices: 33.7 us -> 13.3 us
  between operations: 15 us -> 0.82 us
  matrix products: 24.3 us -> 12.7 us
  local copies, waits for them, and re-layouts: 21.1 us -> 15.7 us
    psum x2 -> x0, waiting for transfers between devices: 59.4 us -> none  [the longest x1 31.6 us: per_device(): side = lax.psum(jnp.concatenate([pts_part, depth_part], 1), 'scen')]
    pallas_call x0 -> x1, Pallas kernels: none -> 50.8 us  [per_device(): pl.pallas_call(functools.partial(step_kernel, n, groups, steps, depth_max...]
    all_to_all x4 -> x0, waiting for transfers between devices: 20.7 us -> none  [per_device(): lax.all_to_all(out.reshape(n, 2, scen, 2 * ends // n), 'rows', 0, 0, tile...]
    all_to_all x4 -> x0, starting transfers between devices: 14.5 us -> none  [per_device(): lax.all_to_all(out.reshape(n, 2, scen, 2 * ends // n), 'rows', 0, 0, tile...]
    all_gather x3 -> x1, blocking collectives: 15.6 us -> 5.25 us  [per_device(): switches = lax.all_gather(switch_bus, 'scen', axis=1, tiled=True)]
    all_to_all x1 -> x0, blocking collectives: 8.94 us -> none  [per_device(): lax.all_to_all(own_current.reshape(scen, n, slots).transpose(1, 0, 2), 'r...]
    reduce_scatter x1 -> x0, waiting for transfers between devices: 8.07 us -> none  [per_device(): voltage = lax.psum_scatter(partial, 'scen', scatter_dimension=0, tiled=True)]
    ppermute x4 -> x0, starting transfers between devices: 7.01 us -> none  [swapped(): return lax.ppermute(value, axis, pairs)]
  transfers between devices with their start and end apart: 13 -> 2, of which waited for: 7 -> 0; matrix products, arithmetic and copies ran while one was open for 17% -> 26% of each run, Pallas kernels for 0% -> 0%
where the time goes in v1:
time: 112 us
  Pallas kernels  50.8 us (45%)
  local copies, waits for them, and re-layouts  15.7 us (14%)
  starting transfers between devices  13.3 us (12%)
  other arithmetic  13.2 us (12%)
  matrix products  12.7 us (11%)
  blocking collectives  5.25 us (5%)
    pallas_call x1, Pallas kernels, per_device(): pl.pallas_call(functools.partial(step_kernel, n, groups, steps, depth_max...  50.8 us
    all_to_all x1, starting transfers between devices, per_device(): lax.all_to_all(jnp.concatenate([bus_out, ends_out], 1), 'rows', 0, 0, til...  7.28 us
    all_to_all x1, starting transfers between devices, per_device(): got = lax.all_to_all(sent, 'rows', 0, 0, tiled=True)  6 us
    all_gather x1, blocking collectives, per_device(): switches = lax.all_gather(switch_bus, 'scen', axis=1, tiled=True)  5.25 us
    dot_general x1, matrix products, per_device(): narrow = jnp.dot(inverse, col_sel, preferred_element_type=f32).astype(bf16)  4.04 us
    dot_general x1, matrix products, per_device(): branch_part = jnp.dot(picks, inverse, preferred_element_type=f32)  4.01 us
    unnamed x7, local copies, waits for them, and re-layouts  3.72 us
    dot_general x3, matrix products, exact_dot(): return jnp.dot(left, right, precision=lax.Precision.HIGHEST)  2.64 us
  transfers between devices with their start and end apart: 2, of which 0 were waited for; matrix products, arithmetic and copies ran while one was open for 26% of the time, Pallas kernels for 0%

profile of v1, /device:TPU:0, one launch (start us, length us, event | category | flops | bytes accessed | tf_op | source)
XLA Modules:
  0.0 111.8 jit_solution(7259038294633664591)
XLA Ops:
  0.7 0.9 convert_reduce_fusion.1
  1.6 0.7 fusion.50
  2.2 0.7 add_bitcast_fusion.1
  3.0 1.0 fusion.30
  4.6 7.3 %all-to-all-start = ((f32[8,1,80]{2,1,0:T(1,128)}), f32[8,1,80]{2,1,0:T(1,128)S(1)}, u32[]{:S(2)}, u32[]{:S(2)}) async-start(f32[8,1,80]{2,1,0:T(1,128)} %bitcast.8), calls=%async_computation | async-start | bytes 8192 | tf_op jit(solution)/shard_map/all_to_all | solution.py:332
  11.9 0.7 broadcast_add_fusion
  12.5 0.7 fusion.47
  13.9 0.7 broadcast_compare_fusion
  14.8 0.8 copy.53
  15.6 5.2 %all_gather.3 = s32[2,64,4]{2,0,1:T(2,128)S(1)} all-gather(s32[2,16,4]{2,0,1:T(2,128)S(1)} %copy.53), channel_id=1, replica_groups=mesh['rows'=8,'scen'=4] {'scen'}, dimensions={1}, use_global_device_ids=true | all-gather | bytes 2560 | tf_op jit(solution)/shard_map/all_gather | solution.py:367
  20.9 0.9 maximum_maximum_fusion
  21.9 0.7 multiply_bitcast_fusion
  22.6 2.2 %concatenate.39 = f32[120,128]{1,0:T(8,128)S(1)} concatenate(f32[1,128]{1,0:T(1,128)} %bitcast.69, f32[1,128]{1,0:T(1,128)S(1)} %multiply_bitcast_fusion, f32[6,128]{1,0:T(8,128)S(1)} %broadcast_in_dim.38, f32[16,128]{1,0:T(8,128)} %param.25, f32[96,128]{1,0:T(8,128)} %bitcast.59), dimensions={0} | concatenate | bytes 122880 | tf_op jit(solution)/shard_map/concatenate | solution.py:348
  25.1 0.7 fusion.42
  26.5 2.5 %dynamic-slice_reduce_fusion.1 = (s32[64]{0:T(128)S(1)}, s32[64]{0:T(128)S(1)}) fusion(s32[2,64,4]{2,0,1:T(2,128)S(1)} %all_gather.3, s32[]{:T(128)S(6)} %select_n.131, s32[]{:T(128)S(6)} %add.245), kind=kLoop, calls=%fused_computation.49 | loop fusion | bytes 1032 | tf_op jit(solution)/shard_map/slice | solution.py:371
  29.0 0.9 and_convert_fusion.home_ref
  29.9 4.0 %multiply_reduce_fusion = (f32[64]{0:T(128)S(1)}, f32[64,2048]{1,0:T(8,128)}) fusion(s32[2048]{0:T(1024)S(1)} %iota_add_fusion, s32[64]{0:T(128)S(1)} %get-tuple-element.3, s32[64]{0:T(128)S(1)} %get-tuple-element.2, bf16[1024,2048]{1,0:T(8,128)(2,1)} %inverse_ref.1, s32[1024]{0:T(1024)S(1)} %iota_add_fusion.1), kind=kOutput, calls=%fused_computation.19 | convolution fusion | flops 269680576 | bytes 4731648 | tf_op jit(solution)/shard_map/dot_general | solution.py:376
  34.6 0.7 broadcast_in_dim.40
  35.3 6.0 %all-to-all-start.1 = ((f32[8,120,64]{1,2,0:T(8,128)}), f32[8,120,64]{1,2,0:T(8,128)S(1)}, u32[]{:S(2)}, u32[]{:S(2)}) async-start(f32[8,120,64]{1,2,0:T(8,128)} %bitcast.20), calls=%async_computation.1 | async-start | bytes 524288 | tf_op jit(solution)/shard_map/all_to_all | solution.py:361
  42.1 4.0 %fusion.7 = bf16[384,1024]{1,0:T(8,128)(2,1)S(1)} fusion(bf16[1024,2048]{1,0:T(8,128)(2,1)} %inverse_ref.1, s32[384]{0:T(512)S(1)} %pad_add_fusion.1), kind=kOutput, calls=%fused_computation.13 | convolution fusion | flops 1612578816 | bytes 4982272 | tf_op jit(solution)/shard_map/dot_general | solution.py:374
  46.5 1.7 %fusion.12.part_ref = bf16[640,384]{1,0:T(8,128)(2,1)} fusion(bf16[384,1024]{1,0:T(8,128)(2,1)S(1)} %fusion.7, s32[1024]{0:T(1024)S(1)} %iota_add_fusion.1, s32[640]{0:T(1024)S(1)} %pad_add_fusion), kind=kOutput, calls=%fused_computation.16 | convolution fusion | flops 504217600 | bytes 1284608 | tf_op jit(solution)/shard_map/dot_general | solution.py:375
  48.8 1.3 %fusion.4.merge_ref = bf16[640,640]{1,0:T(8,128)(2,1)} fusion(s32[640]{0:T(1024)S(1)} %pad_add_fusion, pred[640]{0:T(1024)(128)(4,1)S(1)} %broadcast_compare_fusion.1), kind=kLoop, calls=%fused_computation.10 | loop fusion | flops 1228800 | bytes 822400 | tf_op jit(solution)/shard_map/convert_element_type | solution.py:388
  50.1 1.3 %fusion.15.volt_ref = f32[16,256]{1,0:T(8,128)} fusion(f32[16,2048]{1,0:T(8,128)S(1)} %copy-done, pred[2048,384]{1,0:T(32,128)(4,1)S(1)} %iota_compare_fusion), kind=kOutput, calls=%fused_computation.17 | convolution fusion | flops 100663296 | bytes 671744 | tf_op jit(solution)/shard_map/dot_general | solution.py:21
  51.5 0.7 pad_maximum_fusion.side_ref
  52.2 1.3 %compare_convert_fusion.row_sel_ref = bf16[640,1024]{1,0:T(8,128)(2,1)} fusion(s32[1024]{0:T(1024)S(1)} %iota_add_fusion.1, s32[640]{0:T(1024)S(1)} %pad_add_fusion), kind=kLoop, calls=%fused_computation | loop fusion | flops 1310720 | bytes 1317376 | tf_op jit(solution)/shard_map/convert_element_type | solution.py:373
  53.9 0.7 slice.41.rates_ref
  54.7 0.7 slice.43.state_ref
  55.8 1.0 reshape.278.source_ref
  57.4 0.7 broadcast_in_dim.43.admit_ref
  58.1 50.8 %shard_map.158 = (f32[16,2048]{1,0:T(8,128)}, f32[16,128]{1,0:T(8,128)}) custom-call(bf16[640,384]{1,0:T(8,128)(2,1)} %fusion.12.part_ref, f32[64,512]{1,0:T(8,128)} %pad_maximum_fusion.side_ref, f32[16,256]{1,0:T(8,128)} %fusion.15.volt_ref, f32[136,128]{1,0:T(8,128)} %pad.13.info_ref, f32[8,512]{1,0:T(8,128)} %slice.41.rates_ref, ...), custom_call_target="tpu_custom_call" | custom-call | tf_op jit(solution)/shard_map/pallas_call | solution.py:409
  108.9 1.6 %copy.64 = f32[16,2048]{1,0:T(8,128)} copy(f32[16,2048]{1,0:T(8,128)} %get-tuple-element.10) | data formatting | bytes 262144
  110.5 1.3 %copy.65 = f32[16,128]{1,0:T(8,128)} copy(f32[16,128]{1,0:T(8,128)} %get-tuple-element.11) | data formatting | bytes 16384
  (51 shorter events, 6.7 us)
Async XLA Ops:
  0.6 49.4 %copy-start = (f32[16,2048]{1,0:T(8,128)S(1)}, f32[16,2048]{1,0:T(8,128)}, u32[]{:S(2)}) copy-start(f32[16,2048]{1,0:T(8,128)} %param.16) | copy-start | bytes 393220
  4.6 30.0 %all-to-all-start = ((f32[8,1,80]{2,1,0:T(1,128)}), f32[8,1,80]{2,1,0:T(1,128)S(1)}, u32[]{:S(2)}, u32[]{:S(2)}) async-start(f32[8,1,80]{2,1,0:T(1,128)} %bitcast.8), calls=%async_computation | async-start | bytes 8192 | tf_op jit(solution)/shard_map/all_to_all | solution.py:332
  35.3 18.2 %all-to-all-start.1 = ((f32[8,120,64]{1,2,0:T(8,128)}), f32[8,120,64]{1,2,0:T(8,128)S(1)}, u32[]{:S(2)}, u32[]{:S(2)}) async-start(f32[8,120,64]{1,2,0:T(8,128)} %bitcast.20), calls=%async_computation.1 | async-start | bytes 524288 | tf_op jit(solution)/shard_map/all_to_all | solution.py:361

commit v2 on v1

v2 whole, which is shorter than its diff:
```python
import functools

import jax
import jax.numpy as jnp
import numpy as np
from jax import lax
from jax.experimental import pallas as pl
from jax.experimental.pallas import tpu as pltpu
from jax.sharding import PartitionSpec as P


def split_dot(value, selector):
    rows = value.shape[0]
    high = value.astype(jnp.bfloat16)
    rest = value - high.astype(jnp.float32)
    middle = rest.astype(jnp.bfloat16)
    low = (rest - middle.astype(jnp.float32)).astype(jnp.bfloat16)
    stacked = jnp.concatenate([high, middle, low], 0)
    out = jnp.dot(stacked, selector, preferred_element_type=jnp.float32)
    return out[:rows] + out[rows : 2 * rows] + out[2 * rows :]


def step_kernel(
    n,
    groups,
    steps,
    depth_max,
    cap,
    slots,
    inverse_ref,
    prev_ref,
    meta_ref,
    state_ref,
    source_ref,
    info_ref,
    switch_ref,
    order_ref,
    lanes_ref,
    voltage_ref,
    current_ref,
    bus_out,
    bus_in,
    switch_in,
    model_out,
    model_in,
    col_sel,
    row_sel,
    narrow,
    merge,
    branch_part,
    part,
    side,
    volt_out,
    part_in,
    side_in,
    matrix,
    volt_in,
    info_in,
    line_out,
    line_in,
    feed_out,
    feed_in,
    factor_out,
    factor_in,
    partial_out,
    partial_in,
    state_out,
    state_in,
    group_sems,
    pair_sems,
    line_sems,
    last_sems,
    home_sems,
    bus_sems,
    model_sems,
    switch_sems,
):
    f32, bf16 = jnp.float32, jnp.bfloat16
    place = lax.axis_index("rows")
    share = lax.axis_index("scen")
    subs = n // 2
    subnet, half = place // 2, place % 2
    base_row = subnet * 2
    size = 2 * groups
    me = half * groups + share
    scen = state_ref.shape[0]
    points = matrix.shape[0]
    block = points // size
    lower = half == 0

    def member(index):
        return (base_row + index // groups, index % groups)

    def remote(src, dst, sems, device):
        return pltpu.make_async_remote_copy(
            src_ref=src,
            dst_ref=dst,
            send_sem=sems.at[0],
            recv_sem=sems.at[1],
            device_id=device,
            device_id_type=pl.DeviceIdType.MESH,
        )

    barrier = pltpu.get_barrier_semaphore()
    for d in range(1, size):
        pl.semaphore_signal(
            barrier, inc=1, device_id=member((me + d) % size), device_id_type=pl.DeviceIdType.MESH
        )
    for d in range(1, subs):
        for other in range(2):
            device = (((subnet + d) % subs) * 2 + other, share)
            pl.semaphore_signal(barrier, inc=1, device_id=device, device_id_type=pl.DeviceIdType.MESH)
    pl.semaphore_wait(barrier, size - 1 + 2 * (subs - 1))

    width = inverse_ref.shape[1]
    local = inverse_ref.shape[0]
    models = meta_ref.shape[1]
    ends = lanes_ref.shape[1]
    per_group = 128 // (2 * slots)
    past_rows = depth_max * 2 * scen
    iota = functools.partial(lax.broadcasted_iota, jnp.int32)
    dest = jnp.broadcast_to(meta_ref[0:1, :], (models, models))
    dest_col = dest.T
    same = dest == dest_col
    rows_at, lanes_at = iota((models, models), 0), iota((models, models), 1)
    rank_col = jnp.sum(jnp.where(same & (lanes_at < rows_at), 1.0, 0.0), axis=1, keepdims=True)
    rank_row = jnp.sum(jnp.where(same & (rows_at < lanes_at), 1.0, 0.0), axis=0, keepdims=True)
    dest_col = dest_col[:, 0:1].astype(jnp.int32)
    spot = (dest_col >> 1) * 128 + (dest_col & 1) * slots + rank_col.astype(jnp.int32)
    spot = spot + (place % per_group) * (2 * slots)
    placing = jnp.where(iota((models, subs * 128), 1) == spot, 1.0, 0.0).astype(bf16)
    dest_row = meta_ref[0:1, :].astype(jnp.int32)
    bus_row = meta_ref[1:2, :] + ((dest_row & 1) * width + 1).astype(f32)
    spread = split_dot(jnp.broadcast_to(bus_row, (16, models)), placing)
    for g in range(subs):
        bus_out[g] = spread[:, g * 128 : (g + 1) * 128]
    moved_buses, moved_models = [], []
    for d in range(1, n):
        to = (place + d) % n
        moved_buses.append(remote(bus_out.at[to // 2], bus_in.at[place], bus_sems.at[d], (to, share)))
    for copy in moved_buses:
        copy.start()
    bus_in[place] = bus_out[subnet]
    pair = ((place // 2) * 2 + (1 - half), share)
    info_copy = remote(info_ref, info_in, pair_sems.at[1], pair)
    info_copy.start()
    switches = []
    for d in range(1, groups):
        device = (place, (share + d) % groups)
        switches.append(remote(switch_ref, switch_in.at[d - 1], switch_sems.at[d], device))
    for copy in switches:
        copy.start()
    lag_row = meta_ref[2:3, :]
    gain_row = (1.0 - lag_row) * meta_ref[3:4, :]
    payload = jnp.concatenate(
        [
            jnp.broadcast_to(lag_row, (8, models)),
            jnp.broadcast_to(gain_row, (8, models)),
            state_ref[...],
            source_ref[...],
        ],
        0,
    )
    for g in range(subs):
        model_out[g] = split_dot(payload, placing[:, g * 128 : (g + 1) * 128])
    for d in range(1, n):
        to = (place + d) % n
        moved_models.append(remote(model_out.at[to // 2], model_in.at[place], model_sems.at[d], (to, share)))

    for copy in switches:
        copy.wait()
    blocks = [switch_in[d - 1] for d in range(1, groups)] + [switch_ref[...]]
    scens = groups * scen
    pick_at = jnp.concatenate(blocks, 0).astype(jnp.int32)
    pick_a, pick_b = pick_at[:, 0:1], pick_at[:, 1:2]
    row_ids = iota((scens, local), 1) + share * local
    picks = (jnp.where(row_ids == pick_a, 1.0, 0.0) - jnp.where(row_ids == pick_b, 1.0, 0.0)).astype(bf16)
    tile = min(width, 512)
    depth_part = jnp.zeros((scens, 1), f32)
    for at in range(0, width, tile):
        piece = jnp.dot(picks, inverse_ref[:, at : at + tile], preferred_element_type=f32)
        branch_part[:, at : at + tile] = piece
        col_ids = iota((scens, tile), 1) + (half * width + at)
        signs = jnp.where(col_ids == pick_a, 1.0, 0.0) - jnp.where(col_ids == pick_b, 1.0, 0.0)
        depth_part = depth_part + jnp.sum(piece * signs, axis=1, keepdims=True)

    info_copy.wait()
    for copy in moved_buses:
        copy.wait()

    def gathered(ref):
        pieces = []
        for g in range(n // per_group):
            total = ref[g * per_group]
            for k in range(1, per_group):
                total = total + ref[g * per_group + k]
            pieces.append(total)
        return split_dot(jnp.concatenate(pieces, 1), order_ref[...])

    info = info_ref[...] + info_in[...]
    end_row = jnp.broadcast_to(info[past_rows + 2 : past_rows + 3], (16, ends))
    pts = jnp.concatenate([gathered(bus_in), end_row], 1)
    pts_col = pts.T[:, 0:1].astype(jnp.int32) - 1
    pts = pts[0:1].astype(jnp.int32) - 1
    own_pts = jnp.concatenate(
        [jnp.where(lower, pts[:, :cap], pts[:, cap : 2 * cap]), pts[:, 2 * cap :]], 1
    ) - half * width
    cols = cap + ends
    col_sel[...] = jnp.where(iota((width, cols), 0) == own_pts, 1.0, 0.0).astype(bf16)

    for at in range(0, local, 256):
        rows = slice(at, at + 256)
        narrow[rows, :] = jnp.dot(
            inverse_ref[rows, :], col_sel[...], preferred_element_type=f32
        ).astype(bf16)

    row_sel[...] = jnp.where(iota((points, local), 1) + share * local == pts_col, 1.0, 0.0).astype(bf16)
    part[...] = jnp.dot(row_sel[...], narrow[...], preferred_element_type=f32).astype(bf16)

    first = []
    for d in range(1, size):
        peer = (me + d) % size
        rows = pl.ds(pl.multiple_of(peer * block, 16), block)
        first.append(remote(part.at[rows], part_in.at[d - 1], group_sems.at[0, d], member(peer)))
    for copy in first:
        copy.start()
    side[:, :cols] = jnp.dot(picks, narrow[...], preferred_element_type=f32)
    side[:, cols:] = jnp.broadcast_to(depth_part, (scens, 128))
    sides = []
    for d in range(1, size):
        peer = (me + d) % size
        at = (share + groups - peer % groups + groups - 1) % groups
        rows = pl.ds(pl.multiple_of(at * scen, 8), scen)
        sides.append(remote(side.at[rows], side_in.at[d - 1], group_sems.at[1, d], member(peer)))
    for copy in sides:
        copy.start()
    volt_out[...] = split_dot(prev_ref[...], col_sel[:, :cap])
    volt_copy = remote(volt_out, volt_in, pair_sems.at[0], pair)
    volt_copy.start()
    for copy in moved_models:
        copy.start()
    model_in[place] = model_out[subnet]
    equal = pts == pts_col
    sub_at = iota((points, points), 0)
    leader = jnp.min(jnp.where(equal, sub_at.astype(f32), float(points)), axis=0, keepdims=True)
    leading = leader == iota((1, points), 1).astype(f32)
    merge[...] = jnp.where(equal & leading, 1.0, 0.0).astype(bf16)
    perm = jnp.where(
        iota((ends, ends), 0) == lanes_ref[0:1, :] + subnet * lanes_ref[2:3, :], 1.0, 0.0
    ).astype(bf16)
    own_rows = pl.ds(pl.multiple_of(me * block, 16), block)

    def placed(pieces):
        lows = jnp.zeros_like(pieces[0][1][:, :cap])
        highs = jnp.zeros_like(lows)
        rest = jnp.zeros_like(pieces[0][1][:, cap:])
        for from_lower, piece in pieces:
            lows = lows + jnp.where(from_lower, piece[:, :cap], 0.0)
            highs = highs + jnp.where(from_lower, 0.0, piece[:, :cap])
            rest = rest + piece[:, cap:]
        return lows, highs, rest

    pieces = [(lower, part[own_rows, :].astype(f32))]
    for d in range(1, size):
        first[d - 1].wait()
        pieces.append(((me + size - d) % size < groups, part_in[d - 1].astype(f32)))
    matrix[own_rows, :] = jnp.concatenate(placed(pieces), 1).astype(bf16)
    second = []
    for d in range(1, size):
        second.append(
            remote(matrix.at[own_rows], matrix.at[own_rows], group_sems.at[2, d], member((me + d) % size))
        )
    for copy in second:
        copy.start()

    pieces = [(lower, side[(groups - 1) * scen :, :])]
    for d in range(1, size):
        sides[d - 1].wait()
        pieces.append(((me + size - d) % size < groups, side_in[d - 1]))
    lows, highs, rest = placed(pieces)
    branch = jnp.concatenate([lows, highs, rest[:, :ends]], 1)
    depth = rest[:, ends : ends + 1]
    volt_copy.wait()
    own_volt, other_volt = volt_out[...], volt_in[...]
    volt = jnp.concatenate(
        [jnp.where(lower, own_volt, other_volt), jnp.where(lower, other_volt, own_volt)], 1
    )
    delays = info[past_rows : past_rows + 1]
    impedance = info[past_rows + 1 : past_rows + 2]
    admittance = 2.0 / jnp.where(delays == 0.0, 1.0, impedance)
    history = [info[k * 2 * scen : (k + 1) * 2 * scen] for k in range(depth_max)]
    for copy in moved_models:
        copy.wait()
    received = gathered(model_in)
    lag, gain = received[0:1], received[8:9]
    admit = switch_ref[:, 2:3]
    current = received[16 : 16 + scen]
    lines = []
    homes = []
    for step in range(steps):
        current = lag * current + gain * (received[16 + (step + 1) * scen : 16 + (step + 2) * scen] - volt)
        if step + 1 == steps:
            state_out[...] = jnp.where(lower, current[:, :cap], current[:, cap:])
            for d in range(1, n):
                homes.append(
                    remote(state_out, state_in.at[d - 1], home_sems.at[d], ((place + d) % n, share))
                )
            for copy in homes:
                copy.start()
        if step >= 2:
            for copy in lines[step - 2]:
                copy.wait()
            merged = jnp.zeros((2 * scen, ends), f32)
            for d in range(1, subs):
                moved = split_dot(line_in[step - 2, d - 1], perm)
                merged = merged + jnp.where(lanes_ref[1:2, :] == (subnet + subs - d) % subs, moved, 0.0)
            history.append(merged)
        line_term = jnp.zeros((scen, ends), f32)
        for delay in range(2, depth_max + 1):
            older = history[step - delay + depth_max]
            line_term = line_term + jnp.where(
                delays == delay, -admittance * older[:scen] - older[scen:], 0.0
            )
        feed = split_dot(jnp.concatenate([current, -line_term], 1), merge[...])
        rhs = feed.astype(bf16)
        along = jnp.sum(rhs.astype(f32) * branch, axis=1, keepdims=True)
        factor = admit * along / (1.0 + admit * depth)
        if step == 0:
            for copy in second:
                copy.wait()
        if step + 1 < steps:
            full = jnp.dot(rhs, matrix[...], preferred_element_type=f32) - factor * branch
            volt = full[:, : 2 * cap]
        if step + 2 < steps:
            line_out[step] = jnp.concatenate([full[:, 2 * cap :], line_term], 0)
            lines.append(
                [
                    remote(
                        line_out.at[step],
                        line_in.at[step, d - 1],
                        line_sems.at[step, d],
                        (((subnet + d) % subs) * 2 + half, share),
                    )
                    for d in range(1, subs)
                ]
            )
            for copy in lines[step]:
                copy.start()

    feed_out[...] = rhs
    factor_out[...] = jnp.broadcast_to(factor, factor_out.shape)
    shared = []
    for d in range(1, groups):
        device = (place, (share + d) % groups)
        shared.append(remote(feed_out, feed_in.at[d - 1], last_sems.at[0, d], device))
        shared.append(remote(factor_out, factor_in.at[d - 1], last_sems.at[1, d], device))
    for copy in shared:
        copy.start()
    for copy in shared:
        copy.wait()
    feeds = jnp.concatenate([feed_in[d - 1] for d in range(1, groups)] + [rhs], 0)
    dense = jnp.dot(feeds, row_sel[...], preferred_element_type=f32).astype(bf16)
    for at in range(0, width, tile):
        product = jnp.dot(dense, inverse_ref[:, at : at + tile], preferred_element_type=f32)
        for d in range(1, groups):
            rows = slice((d - 1) * scen, d * scen)
            partial_out[d - 1, :, at : at + tile] = (
                product[(d - 1) * scen : d * scen]
                - factor_in[d - 1][:, 0:1] * branch_part[rows, at : at + tile]
            )
        rows = slice((groups - 1) * scen, scens)
        voltage_ref[:, at : at + tile] = (
            product[(groups - 1) * scen :] - factor * branch_part[rows, at : at + tile]
        )
    partials = []
    for d in range(1, groups):
        device = (place, (share + groups - d) % groups)
        partials.append(remote(partial_out.at[d - 1], partial_in.at[d - 1], last_sems.at[2, d], device))
    for copy in partials:
        copy.start()
    for copy in homes:
        copy.wait()
    back = jnp.concatenate([state_out[...]] + [state_in[d - 1] for d in range(1, n)], 0)
    home = jnp.where(
        iota((cap, models), 0) == place * slots + rank_row.astype(jnp.int32), 1.0, 0.0
    ).astype(bf16)
    back = split_dot(back, home)
    out = jnp.zeros((scen, models), f32)
    for d in range(n):
        out = out + jnp.where(dest_row == (place + n - d) % n, back[d * scen : (d + 1) * scen], 0.0)
    current_ref[...] = out
    for copy in partials:
        copy.wait()
    total = voltage_ref[...]
    for d in range(1, groups):
        total = total + partial_in[d - 1]
    voltage_ref[...] = total


def per_device(
    inverse,
    voltage_prev,
    line_delay,
    line_bus,
    line_impedance,
    line_past,
    model_dest,
    model_bus,
    model_gain,
    model_lag,
    model_state,
    model_source,
    switch_bus,
    switch_admittance,
):
    n = lax.axis_size("rows")
    groups = lax.axis_size("scen")
    place = lax.axis_index("rows")
    share = lax.axis_index("scen")
    subnet = place // 2
    half = place % 2
    lower = half == 0
    depth_rows, width = inverse.shape
    scen = voltage_prev.shape[0]
    steps = model_source.shape[0]
    ends = line_bus.shape[1]
    models = model_bus.shape[0]
    depth_max = line_past.shape[0]
    slots = max(2, 2 * models // n)
    cap = n * slots
    f32, bf16 = jnp.float32, jnp.bfloat16

    pad = max(128, 2 * ends)
    points = 2 * cap + pad

    def end_lanes(values):
        none = jnp.zeros((values.shape[0], ends), values.dtype)
        both = jnp.where(
            lower, jnp.concatenate([values, none], 1), jnp.concatenate([none, values], 1)
        )
        return jnp.pad(both, ((0, 0), (0, pad - 2 * ends)))

    meta = jnp.stack([model_dest[:, 0].astype(f32), model_bus.astype(f32), model_lag, model_gain])
    meta = jnp.pad(meta, ((0, 4), (0, 0)))
    past = line_past[:, :, :, 0, :].reshape(depth_max * 2 * scen, ends)
    global_bus = (line_bus + half * width + 1).astype(f32)
    info = end_lanes(
        jnp.concatenate(
            [past, line_delay.astype(f32), line_impedance, global_bus, jnp.zeros((5, ends), f32)], 0
        )
    )
    switch_at = lax.dynamic_index_in_dim(switch_bus, subnet, axis=2, keepdims=False)
    admit = lax.dynamic_index_in_dim(switch_admittance, subnet, axis=1, keepdims=False)
    switch = jnp.stack([switch_at[0].astype(f32), switch_at[1].astype(f32), admit], 1)
    switch = jnp.pad(switch, ((0, 0), (0, 125)))

    lane = np.arange(2 * cap)
    comes = lane % cap // slots * 2 * slots + lane // cap * slots + lane % slots
    order = jnp.asarray(np.arange(2 * cap)[:, None] == comes[None, :], bf16)
    per_pair = ends // n
    lane = np.arange(pad)
    partner = lane % ends // per_pair
    origin = partner % 2 * ends + lane // ends * per_pair + lane % ends % per_pair
    live = lane < 2 * ends
    lanes = np.zeros((8, pad), np.int32)
    lanes[0] = np.where(live, origin, -1)
    lanes[1] = partner // 2
    lanes[2] = np.where(live, 2 * per_pair, 0)
    lanes = jnp.asarray(lanes)

    size = 2 * groups
    cols = cap + pad
    count = 16 + (steps + 1) * scen
    vmem = pl.BlockSpec(memory_space=pltpu.VMEM)
    voltage, model_current = pl.pallas_call(
        functools.partial(step_kernel, n, groups, steps, depth_max, cap, slots),
        out_shape=(
            jax.ShapeDtypeStruct((scen, width), f32),
            jax.ShapeDtypeStruct((scen, models), f32),
        ),
        in_specs=[vmem] * 9,
        out_specs=(vmem, vmem),
        scratch_shapes=[
            pltpu.VMEM((n // 2, 16, 128), f32),
            pltpu.VMEM((n, 16, 128), f32),
            pltpu.VMEM((groups - 1, scen, 128), f32),
            pltpu.VMEM((n // 2, count, 128), f32),
            pltpu.VMEM((n, count, 128), f32),
            pltpu.VMEM((width, cols), bf16),
            pltpu.VMEM((points, depth_rows), bf16),
            pltpu.VMEM((depth_rows, cols), bf16),
            pltpu.VMEM((points, points), bf16),
            pltpu.VMEM((groups * scen, width), f32),
            pltpu.VMEM((points, cols), bf16),
            pltpu.VMEM((groups * scen, cols + 128), f32),
            pltpu.VMEM((scen, cap), f32),
            pltpu.VMEM((size - 1, points // size, cols), bf16),
            pltpu.VMEM((size - 1, scen, cols + 128), f32),
            pltpu.VMEM((points, points), bf16),
            pltpu.VMEM((scen, cap), f32),
            pltpu.VMEM(info.shape, f32),
            pltpu.VMEM((steps - 2, 2 * scen, pad), f32),
            pltpu.VMEM((steps - 2, n // 2 - 1, 2 * scen, pad), f32),
            pltpu.VMEM((scen, points), bf16),
            pltpu.VMEM((groups - 1, scen, points), bf16),
            pltpu.VMEM((scen, 128), f32),
            pltpu.VMEM((groups - 1, scen, 128), f32),
            pltpu.VMEM((groups - 1, scen, width), f32),
            pltpu.VMEM((groups - 1, scen, width), f32),
            pltpu.VMEM((scen, cap), f32),
            pltpu.VMEM((n - 1, scen, cap), f32),
            pltpu.SemaphoreType.DMA((3, size, 2)),
            pltpu.SemaphoreType.DMA((2, 2)),
            pltpu.SemaphoreType.DMA((steps - 2, n // 2, 2)),
            pltpu.SemaphoreType.DMA((3, groups, 2)),
            pltpu.SemaphoreType.DMA((n, 2)),
            pltpu.SemaphoreType.DMA((n, 2)),
            pltpu.SemaphoreType.DMA((n, 2)),
            pltpu.SemaphoreType.DMA((groups, 2)),
        ],
        compiler_params=pltpu.CompilerParams(
            collective_id=0, has_side_effects=True, vmem_limit_bytes=56 * 2**20
        ),
    )(
        inverse,
        voltage_prev,
        meta,
        model_state,
        model_source.reshape(steps * scen, models),
        info,
        switch,
        order,
        lanes,
    )
    return (voltage, model_current)


def solution(mesh):
    placed = (
        P("scen", "rows"),
        P("scen", "rows"),
        P("rows", None),
        P("rows", None),
        P("rows", None),
        P(None, None, "scen", "rows", None),
        P("rows", None),
        P("rows"),
        P("rows"),
        P("rows"),
        P("scen", "rows"),
        P(None, "scen", "rows"),
        P(None, "scen", None),
        P("scen", None),
    )
    return jax.shard_map(
        per_device,
        mesh=mesh,
        in_specs=placed,
        out_specs=(P("scen", "rows"), P("scen", "rows")),
        check_vma=False,
    )
```

time: 112 us -> 75.5 us (0.67)
  starting transfers between devices: 13.3 us -> 0 us
  Pallas kernels: 50.8 us -> 64.1 us
  matrix products: 12.7 us -> 0 us
  local copies, waits for them, and re-layouts: 15.7 us -> 5.72 us
  other arithmetic: 13.2 us -> 4.7 us
  blocking collectives: 5.25 us -> 0 us
    pallas_call x1, Pallas kernels: 50.8 us -> 64.1 us  [per_device(): pl.pallas_call(functools.partial(step_kernel, n, groups, steps, depth_max...]
    all_to_all x2 -> x0, starting transfers between devices: 13.3 us -> none  [the longest x1 7.28 us: per_device(): lax.all_to_all(jnp.concatenate([bus_out, ends_out], 1), 'rows', 0, 0, til...]
    dot_general x7 -> x0, matrix products: 12.7 us -> none  [the longest x1 4.04 us: per_device(): narrow = jnp.dot(inverse, col_sel, preferred_element_type=f32).astype(bf16)]
    all_gather x1 -> x0, blocking collectives: 5.25 us -> none  [per_device(): switches = lax.all_gather(switch_bus, 'scen', axis=1, tiled=True)]
    slice x9 -> x0, local copies, waits for them, and re-layouts: 4.9 us -> none  [the longest x1 2.51 us: per_device(): switches[0][:, None]]
    broadcast_in_dim x9 -> x1, local copies, waits for them, and re-layouts: 2.75 us -> 0.01 us  [per_device(): jnp.zeros((5, ends), f32)]
    concatenate x5 -> x0, other arithmetic: 2.33 us -> none  [the longest x1 0.93 us: per_device(): jnp.concatenate([past, line_delay.astype(f32), line_impedance, jnp.zeros(...]
    convert_element_type x4 -> x3, other arithmetic: 4.16 us -> 2.03 us  [the longest x1 0.71 us: per_device(): switch_at[0].astype(f32)]
  transfers between devices with their start and end apart: 2 -> 0, of which waited for: 0 -> 0; matrix products, arithmetic and copies ran while one was open for 26% -> 0% of each run, Pallas kernels for 0% -> 0%
where the time goes in v2:
time: 75.5 us; the launch traced here: 75.2 us
  Pallas kernels  64.1 us (85%)
  local copies, waits for them, and re-layouts  5.72 us (8%)
  other arithmetic  4.7 us (6%)
    pallas_call x1, Pallas kernels, per_device(): pl.pallas_call(functools.partial(step_kernel, n, groups, steps, depth_max...  64.1 us
    unnamed x4, local copies, waits for them, and re-layouts  2.87 us
    another operation x2, other arithmetic, per_device(): jnp.stack([model_dest[:, 0].astype(f32), model_bus.astype(f32), model_lag...  1.92 us
    concatenate x1, local copies, waits for them, and re-layouts, per_device(): jnp.concatenate([past, line_delay.astype(f32), line_impedance, global_bus...  1.52 us

profile of v2, /device:TPU:0, one launch (start us, length us, event | category | flops | bytes accessed | tf_op | source)
XLA Modules:
  0.0 75.2 jit_solution(7578128172545090172)
XLA Ops:
  0.6 0.0 copy-start
  0.7 0.7 add_convert_fusion
  1.3 0.7 convert_element_type.57
  2.0 0.7 convert_bitcast_fusion.1
  2.6 0.7 convert_bitcast_fusion
  3.3 0.0 copy-done
  3.3 0.7 fusion.3
  4.0 1.3 %select_maximum_fusion.meta_ref = f32[8,128]{1,0:T(8,128)} fusion(f32[1,128]{1,0:T(1,128)} %bitcast.14, f32[1,128]{1,0:T(1,128)} %bitcast.15, f32[1,128]{1,0:T(1,128)S(1)} %convert_bitcast_fusion, f32[1,128]{1,0:T(1,128)S(1)} %convert_bitcast_fusion.1), kind=kLoop, calls=%fused_computation.1 | loop fusion | flops 8192 | bytes 6144 | tf_op jit(solution)/shard_map/stack | solution.py:443
  5.3 0.1 copy.30
  5.4 0.6 pad.16.switch_ref
  6.0 1.5 %concatenate.9 = f32[136,16]{1,0:T(8,128)S(1)} concatenate(f32[128,16]{1,0:T(8,128)} %bitcast.12, f32[1,16]{1,0:T(1,128)S(1)} %convert_element_type.57, f32[1,16]{1,0:T(1,128)} %param.20, f32[1,16]{1,0:T(1,128)S(1)} %add_convert_fusion, f32[5,16]{1,0:T(8,128)S(1)} %broadcast_in_dim.4), dimensions={0} | concatenate | bytes 17408 | tf_op jit(solution)/shard_map/concatenate | solution.py:448
  7.5 0.1 pad_select_fusion
  7.6 0.6 pad.15.info_ref
  8.2 64.1 %shard_map.167 = (f32[16,2048]{1,0:T(8,128)}, f32[16,128]{1,0:T(8,128)}) custom-call(bf16[1024,2048]{1,0:T(8,128)(2,1)} %inverse_ref.1, f32[16,2048]{1,0:T(8,128)} %prev_ref.1, f32[8,128]{1,0:T(8,128)} %select_maximum_fusion.meta_ref, f32[16,128]{1,0:T(8,128)} %state_ref.1, f32[96,128]{1,0:T(8,128)} %bitcast.13, f32[136,128]{1,0:T(8,128)} %pad.15.info_ref, ...), custom_call_target="tpu_custom_call" | custom-call | tf_op jit(solution)/shard_map/pallas_call | solution.py:475
  72.3 1.6 %copy.33 = f32[16,2048]{1,0:T(8,128)} copy(f32[16,2048]{1,0:T(8,128)} %get-tuple-element.6) | data formatting | bytes 262144
  73.9 1.3 %copy.34 = f32[16,128]{1,0:T(8,128)} copy(f32[16,128]{1,0:T(8,128)} %get-tuple-element.7) | data formatting | bytes 16384
  (3 shorter events, 0.0 us)
Async XLA Ops:
  0.6 2.7 %copy-start = (f32[16,4]{0,1:T(4,128)S(1)}, f32[16,4]{0,1:T(4,128)}, u32[]{:S(2)}) copy-start(f32[16,4]{0,1:T(4,128)} %param.29) | copy-start | bytes 772
